TPU v7x, 256 devices: a whole 4x4x8 slice. The times are simulated.
256 devices in a mesh: seq: 64 (over z, x, core), grp: 4 (over y).
Axes of the slice: x: 4, y: 4, z: 8, core: 2. Of those that a mesh axis runs over, the one named last changes fastest.
Arguments:
- streams: float32 [3, 16384, 4096], P(None, 'seq', 'grp'), may hold values from -6 to 6
- short_filters: float32 [3, 3, 4096], P(None, None, 'grp'), may hold values from -3.5 to 3.5
- skip_gain: float32 [4096], P('grp'), may hold values from -4 to 4
- long_filter: float32 [16384, 256], P('seq', 'grp'), may hold values from -0.046875 to 0.046875
Outputs:
- hyena_output: float32 [256, 64, 4096], P('seq', None, 'grp')
All inputs are finite; a program needn't handle non-finite values.
Results may differ from a plain program's by a relative error of at most 0.00011.
Values sent between devices are 32-bit elements; how exact they have to be, the bound alone decides.
A program may use at most 64 MiB of HBM per device.

v0:
```python
import functools

import jax
import jax.numpy as jnp
import ml_dtypes
import numpy as np
from jax import lax
from jax.experimental import pallas as pl
from jax.experimental.pallas import tpu as pltpu
from jax.sharding import PartitionSpec as P

MESH = pl.DeviceIdType.MESH
SEQ = 64
GRP = 4
TOK = 256
CH = 1024
POINTS = SEQ * TOK
QUARTERS = 4
LANES = 128


def split_parts(matrix):
    high = matrix.astype(ml_dtypes.bfloat16)
    low = (matrix - high.astype(np.float64)).astype(ml_dtypes.bfloat16)
    return high, low


@functools.cache
def tables():
    r = np.arange(SEQ)
    k1 = np.arange(SEQ)
    m = np.arange(TOK)
    k2 = np.arange(TOK)
    column = np.arange(TOK)
    m_of = 4 * (column % 64) + 2 * ((column // 64) % 2) + column // 128
    coarse = 2 * np.pi * np.outer(k1 + 0.25, r) / SEQ
    head = np.concatenate([np.cos(coarse), -np.sin(coarse)], axis=0)
    head_high, head_low = split_parts(head)
    head_all = np.concatenate([head_high, head_high, head_low], axis=1)
    tail = np.concatenate([np.cos(coarse.T), -np.sin(coarse.T)], axis=1)
    tail_high, tail_low = split_parts(tail)
    tail_all = np.concatenate([tail_high, tail_high, tail_low], axis=1)
    twist = 2 * np.pi * np.outer(k1 + 0.25, m) / POINTS
    turn = 2 * np.pi * np.outer(k1 + 0.25, m_of) / POINTS
    twists = np.stack(
        [np.cos(twist), -np.sin(twist), np.cos(turn) / POINTS, np.sin(turn) / POINTS]
    ).astype(np.float32)
    fine = 2 * np.pi * (np.outer(m, k2) % TOK) / TOK
    fine_cos, fine_sin = np.cos(fine), -np.sin(fine)
    forward = np.block([[fine_cos, fine_sin], [-fine_sin, fine_cos]])
    back = 2 * np.pi * (np.outer(k2, m_of) % TOK) / TOK
    back_cos, back_sin = np.cos(back), np.sin(back)
    inverse = np.block([[back_cos, back_sin], [-back_sin, back_cos]])
    wide = np.stack([*split_parts(forward), *split_parts(inverse)])
    return head_all, tail_all, twists, wide


def halves(values):
    high = values.astype(jnp.bfloat16)
    low = (values - high.astype(jnp.float32)).astype(jnp.bfloat16)
    return high, low


def product(left, right):
    return jnp.dot(left, right, preferred_element_type=jnp.float32)


def kernel(
    streams_hbm, taps_hbm, gain_hbm, filter_hbm, head_hbm, tail_hbm, twist_hbm, wide_hbm,
    out_ref,
    stream, taps, gain, filt, head, tail, twist, wide,
    rim_send, rim_recv, filt_send, filt_recv, filt_all, response,
    gate_send, gate_recv, query_send, query_recv, conv_send, conv_recv,
    load_sem, rim_sems, filt_sems, ring_sems, gate_out, gate_in, query_sems, conv_out, conv_in,
):
    me = lax.axis_index("seq")
    group = lax.axis_index("grp")
    barrier = pltpu.get_barrier_semaphore()

    def greet(step, carry):
        other = lax.rem(me + step, SEQ)
        pl.semaphore_signal(barrier, inc=1, device_id=(other, group), device_id_type=MESH)
        return carry

    def greet_group(step, carry):
        other = lax.rem(group + step, GRP)
        pl.semaphore_signal(barrier, inc=1, device_id=(me, other), device_id_type=MESH)
        return carry

    def load(source, target, slot):
        return pltpu.make_async_copy(source, target, load_sem.at[slot])

    def stream_load(block):
        lanes = pl.ds(block * LANES, LANES)
        return load(streams_hbm.at[:, :, lanes], stream.at[:, block, pl.ds(8, TOK), :], block)

    for block in range(8):
        stream_load(block).start()
    small_loads = [
        load(filter_hbm, filt, 8),
        load(taps_hbm, taps, 9),
        load(gain_hbm, gain, 10),
        load(head_hbm, head, 11),
        load(tail_hbm, tail, 12),
        load(twist_hbm, twist, 13),
        load(wide_hbm, wide, 14),
    ]
    for copy in small_loads:
        copy.start()
    lax.fori_loop(1, SEQ, greet, 0)
    lax.fori_loop(1, GRP, greet_group, 0)

    small_loads[0].wait()
    for half in range(2):
        turned = jnp.transpose(filt[pl.ds(half * LANES, LANES), :])
        filt_send[:, half, :] = turned
    for block in range(8):
        stream_load(block).wait()
    rim_send[...] = jnp.zeros_like(rim_send)
    for s in range(3):
        rim_send[:, pl.ds(2 * s, 2), :] = stream[s, :, pl.ds(TOK + 6, 2), :]
    pl.semaphore_wait(barrier, SEQ - 1 + GRP - 1)

    def rim_copy(other):
        return pltpu.make_async_remote_copy(
            src_ref=rim_send, dst_ref=rim_recv, send_sem=rim_sems.at[0], recv_sem=rim_sems.at[1],
            device_id=(other, group), device_id_type=MESH,
        )

    @pl.when(me < SEQ - 1)
    def _():
        rim_copy(me + 1).start()

    def send_filter(step, carry):
        other = lax.rem(me + step, SEQ)
        pltpu.make_async_remote_copy(
            src_ref=filt_send.at[other], dst_ref=filt_recv.at[me],
            send_sem=filt_sems.at[0], recv_sem=filt_sems.at[1],
            device_id=(other, group), device_id_type=MESH,
        ).start()
        return carry

    lax.fori_loop(1, SEQ, send_filter, 0)
    filt_recv[me] = filt_send[me]
    small_loads[1].wait()

    def feature(s, start, block, size, stride=None):
        lanes = pl.ds(pl.multiple_of(block * LANES, LANES), LANES)

        def rows(first):
            window = pl.ds(first, size) if stride is None else pl.ds(first, size, stride)
            return stream[s, block, window, :]

        return (
            taps[s, 0:1, lanes] * rows(start)
            + taps[s, 1:2, lanes] * rows(start - 1)
            + taps[s, 2:3, lanes] * rows(start - 2)
        )

    def gate(quarter, half):
        for pair in range(2):
            block = quarter * 2 + pair
            first = 8 + half * LANES
            gated = feature(1, first, block, LANES) * feature(2, first, block, LANES)
            turned = jnp.transpose(gated)
            for own in range(2):
                row = half * 4 + pair * 2 + own
                gate_send[quarter, pl.ds(row, SEQ, 8), :] = turned[own * 64 : own * 64 + 64]

    def gate_late(quarter, carry):
        gate(quarter, 1)
        return carry

    lax.fori_loop(0, QUARTERS, gate_late, 0)

    @pl.when(me > 0)
    def _():
        rim_copy(me).wait_recv()
        for s in range(3):
            stream[s, :, pl.ds(6, 2), :] = rim_recv[:, pl.ds(2 * s, 2), :]

    @pl.when(me == 0)
    def _():
        for s in range(3):
            stream[s, :, pl.ds(6, 2), :] = jnp.zeros((8, 2, LANES), jnp.float32)

    def gate_early(quarter, carry):
        gate(quarter, 0)

        def send(step, inner):
            other = lax.rem(me + step, SEQ)
            pltpu.make_async_remote_copy(
                src_ref=gate_send.at[quarter, pl.ds(pl.multiple_of(other * 8, 8), 8)],
                dst_ref=gate_recv.at[quarter, pl.ds(pl.multiple_of(me * 8, 8), 8)],
                send_sem=gate_out.at[quarter], recv_sem=gate_in.at[quarter],
                device_id=(other, group), device_id_type=MESH,
            ).start()
            return inner

        lax.fori_loop(1, SEQ, send, 0)
        own = pl.ds(pl.multiple_of(me * 8, 8), 8)
        gate_recv[quarter, own, :] = gate_send[quarter, own, :]
        return carry

    lax.fori_loop(0, QUARTERS, gate_early, 0)

    def query(block, carry):
        for low in range(4):
            featured = feature(0, 8 + low, block, SEQ, 4)
            query_send[pl.ds(low * 8 + block, SEQ, 32), :] = featured
        return carry

    lax.fori_loop(0, 8, query, 0)

    def send_query(step, carry):
        other = lax.rem(me + step, SEQ)
        pltpu.make_async_remote_copy(
            src_ref=query_send.at[pl.ds(pl.multiple_of(other * 32, 32), 32)],
            dst_ref=query_recv.at[pl.ds(pl.multiple_of(me * 32, 32), 32)],
            send_sem=query_sems.at[0], recv_sem=query_sems.at[1],
            device_id=(other, group), device_id_type=MESH,
        ).start()
        return carry

    lax.fori_loop(1, SEQ, send_query, 0)
    own_query = pl.ds(pl.multiple_of(me * 32, 32), 32)
    query_recv[own_query, :] = query_send[own_query, :]

    def wait_bytes(ref, sem):
        pltpu.make_async_copy(ref, ref, sem).wait()

    wait_bytes(filt_recv.at[pl.ds(0, SEQ - 1)], filt_sems.at[1])
    for half in range(2):
        filt_all[group, :, half * LANES : half * LANES + LANES] = filt_recv[:, half, :]

    def send_ring(step, carry):
        other = lax.rem(group + step, GRP)
        pltpu.make_async_remote_copy(
            src_ref=filt_all.at[group], dst_ref=filt_all.at[group],
            send_sem=ring_sems.at[0], recv_sem=ring_sems.at[1],
            device_id=(me, other), device_id_type=MESH,
        ).start()
        return carry

    lax.fori_loop(1, GRP, send_ring, 0)
    for copy in small_loads[2:]:
        copy.wait()

    def spectrum(rows_of):
        reals, imags = [], []
        for f in range(4):
            high, low = halves(rows_of(f))
            coarse = product(head[...], jnp.concatenate([high, low, high], axis=0))
            real, imag = coarse[:SEQ], coarse[SEQ:]
            reals.append(real * twist[0] - imag * twist[1])
            imags.append(real * twist[1] + imag * twist[0])
        both = jnp.concatenate(
            [jnp.concatenate(reals, axis=0), jnp.concatenate(imags, axis=0)], axis=1
        )
        high, low = halves(both)
        return product(high, wide[0]) + product(low, wide[0]) + product(high, wide[1])

    wait_bytes(filt_all.at[pl.ds(0, GRP - 1)], ring_sems.at[1])
    response[...] = spectrum(lambda f: filt_all[f])

    def convolve(quarter, carry):
        wait_bytes(gate_recv.at[quarter, pl.ds(0, (SEQ - 1) * 8)], gate_in.at[quarter])

        def rows_of(f):
            return jnp.concatenate(
                [gate_recv[quarter, pl.ds(f, SEQ, 8), :], gate_recv[quarter, pl.ds(4 + f, SEQ, 8), :]],
                axis=1,
            )

        signal = spectrum(rows_of)
        reals, imags = [], []
        for f in range(4):
            rows = slice(f * SEQ, f * SEQ + SEQ)
            real, imag = signal[rows, :TOK], signal[rows, TOK:]
            skip = gain[(quarter * 4 + f) * SEQ + me]
            tap_real = response[rows, :TOK] + skip
            tap_imag = response[rows, TOK:]
            reals.append(real * tap_real - imag * tap_imag)
            imags.append(real * tap_imag + imag * tap_real)
        both = jnp.concatenate(
            [jnp.concatenate(reals, axis=0), jnp.concatenate(imags, axis=0)], axis=1
        )
        high, low = halves(both)
        back = product(high, wide[2]) + product(low, wide[2]) + product(high, wide[3])
        for f in range(4):
            rows = slice(f * SEQ, f * SEQ + SEQ)
            real, imag = back[rows, :TOK], back[rows, TOK:]
            turned = jnp.concatenate(
                [real * twist[2] - imag * twist[3], real * twist[3] + imag * twist[2]], axis=0
            )
            high, low = halves(turned)
            result = product(tail[...], jnp.concatenate([high, low, high], axis=0))
            stacked = jnp.concatenate([result[:, :LANES], result[:, LANES:]], axis=0)
            flipped = jnp.transpose(stacked)
            for upper in range(2):
                conv_send[quarter, pl.ds(upper * 4 + f, SEQ, 8), :] = flipped[
                    upper * 64 : upper * 64 + 64
                ]

        def send(step, inner):
            other = lax.rem(me + step, SEQ)
            pltpu.make_async_remote_copy(
                src_ref=conv_send.at[quarter, pl.ds(pl.multiple_of(other * 8, 8), 8)],
                dst_ref=conv_recv.at[quarter, pl.ds(pl.multiple_of(me * 8, 8), 8)],
                send_sem=conv_out.at[quarter], recv_sem=conv_in.at[quarter],
                device_id=(other, group), device_id_type=MESH,
            ).start()
            return inner

        lax.fori_loop(1, SEQ, send, 0)
        own = pl.ds(pl.multiple_of(me * 8, 8), 8)
        conv_recv[quarter, own, :] = conv_send[quarter, own, :]
        return carry

    lax.fori_loop(0, QUARTERS, convolve, 0)

    wait_bytes(query_recv.at[pl.ds(0, (SEQ - 1) * 32)], query_sems.at[1])

    def finish(quarter, carry):
        wait_bytes(conv_recv.at[quarter, pl.ds(0, (SEQ - 1) * 8)], conv_in.at[quarter])
        for pair in range(2):
            block = quarter * 2 + pair
            lanes = pl.ds(pl.multiple_of(block * LANES, LANES), LANES)
            for upper in range(2):
                gathered = jnp.concatenate(
                    [conv_recv[quarter, pl.ds(upper * 4 + pair * 2 + own, SEQ, 8), :] for own in range(2)],
                    axis=0,
                )
                result = jnp.transpose(gathered)
                for lower in range(2):
                    offset = upper * 2 + lower
                    asked = query_recv[pl.ds(offset * 8 + block, SEQ, 32), :]
                    out_ref[offset, :, lanes] = asked * result[lower * 64 : lower * 64 + 64]
        return carry

    lax.fori_loop(0, QUARTERS, finish, 0)

    @pl.when(me < SEQ - 1)
    def _():
        rim_copy(me + 1).wait_send()

    wait_bytes(filt_send.at[pl.ds(0, SEQ - 1)], filt_sems.at[0])
    wait_bytes(filt_all.at[pl.ds(0, GRP - 1)], ring_sems.at[0])
    wait_bytes(query_send.at[pl.ds(0, (SEQ - 1) * 32)], query_sems.at[0])
    for quarter in range(QUARTERS):
        wait_bytes(gate_send.at[quarter, pl.ds(0, (SEQ - 1) * 8)], gate_out.at[quarter])
        wait_bytes(conv_send.at[quarter, pl.ds(0, (SEQ - 1) * 8)], conv_out.at[quarter])


def body(streams, short_filters, skip_gain, long_filter):
    head_all, tail_all, twists, wide = tables()
    dma = pltpu.SemaphoreType.DMA
    f32 = jnp.float32
    any_space = pl.BlockSpec(memory_space=pl.ANY)
    return pl.pallas_call(
        kernel,
        out_shape=jax.ShapeDtypeStruct((TOK // SEQ, SEQ, CH), f32),
        in_specs=[any_space] * 8,
        out_specs=pl.BlockSpec(memory_space=pltpu.VMEM),
        scratch_shapes=[
            pltpu.VMEM((3, 8, TOK + 8, LANES), f32),
            pltpu.VMEM((3, 3, CH), f32),
            pltpu.SMEM((CH,), f32),
            pltpu.VMEM((TOK, 64), f32),
            pltpu.VMEM(head_all.shape, jnp.bfloat16),
            pltpu.VMEM(tail_all.shape, jnp.bfloat16),
            pltpu.VMEM(twists.shape, f32),
            pltpu.VMEM(wide.shape, jnp.bfloat16),
            pltpu.VMEM((8, 8, LANES), f32),
            pltpu.VMEM((8, 8, LANES), f32),
            pltpu.VMEM((SEQ, 2, LANES), f32),
            pltpu.VMEM((SEQ, 2, LANES), f32),
            pltpu.VMEM((GRP, SEQ, TOK), f32),
            pltpu.VMEM((TOK, 2 * TOK), f32),
            pltpu.VMEM((QUARTERS, SEQ * 8, LANES), f32),
            pltpu.VMEM((QUARTERS, SEQ * 8, LANES), f32),
            pltpu.VMEM((SEQ * 32, LANES), f32),
            pltpu.VMEM((SEQ * 32, LANES), f32),
            pltpu.VMEM((QUARTERS, SEQ * 8, LANES), f32),
            pltpu.VMEM((QUARTERS, SEQ * 8, LANES), f32),
            dma((15,)),
            dma((2,)),
            dma((2,)),
            dma((2,)),
            dma((QUARTERS,)),
            dma((QUARTERS,)),
            dma((2,)),
            dma((QUARTERS,)),
            dma((QUARTERS,)),
        ],
        compiler_params=pltpu.CompilerParams(
            collective_id=0, has_side_effects=True, vmem_limit_bytes=48 << 20
        ),
    )(streams, short_filters, skip_gain, long_filter, head_all, tail_all, twists, wide)


def solution(mesh):
    return jax.shard_map(
        body,
        mesh=mesh,
        in_specs=(P(None, "seq", "grp"), P(None, None, "grp"), P("grp"), P("seq", "grp")),
        out_specs=P("seq", None, "grp"),
        check_vma=False,
    )
```

profile of v0, /device:TPU:1, one launch (start us, length us, event | category | flops | bytes accessed | tf_op | source)
XLA Modules:
  0.0 92.2 jit_solution(13203789256958290150)
XLA Ops:
  0.0 0.9 %copy.9.filter_hbm = f32[256,64]{1,0:T(8,128)S(1)} copy(f32[256,64]{0,1:T(8,128)} %param.11) | data formatting | bytes 131072 | tf_op args[3]
  0.9 0.0 copy-start
  0.9 1.6 %copy-done = bf16[4,512,512]{2,1,0:T(8,128)(2,1)S(1)} copy-done((bf16[4,512,512]{2,1,0:T(8,128)(2,1)S(1)}, bf16[4,512,512]{2,1,0:T(8,128)(2,1)}, u32[]{:S(2)}) %copy-start) | copy-done | bytes 2097176
  2.5 0.0 copy-start.1
  2.5 0.9 %copy-done.1 = f32[4,64,256]{2,1,0:T(8,128)S(1)} copy-done((f32[4,64,256]{2,1,0:T(8,128)S(1)}, f32[4,64,256]{2,1,0:T(8,128)}, u32[]{:S(2)}) %copy-start.1) | copy-done | bytes 262168
  3.5 0.0 copy-start.2
  3.5 0.8 copy-done.2
  4.3 0.0 copy-start.3
  4.3 0.8 copy-done.3
  5.1 0.0 copy-start.4
  5.1 0.8 copy-done.4
  5.9 0.0 copy-start.5
  5.9 0.7 copy-done.5
  6.6 84.6 %shard_map.82 = f32[4,64,1024]{2,1,0:T(8,128)S(1)} custom-call(f32[3,256,1024]{2,1,0:T(8,128)} %streams_hbm.1, f32[3,3,1024]{2,1,0:T(4,128)S(1)} %copy-done.3, f32[1024]{0:T(1024)S(1)} %copy-done.5, f32[256,64]{1,0:T(8,128)S(1)} %copy.9.filter_hbm, bf16[128,192]{1,0:T(8,128)(2,1)S(1)} %copy-done.2, bf16[64,384]{1,0:T(8,128)(2,1)S(1)} %copy-done.4, ...), custom_call_target="tpu_custom_call" | custom-call | tf_op jit(solution)/shard_map/pallas_call | solution.py:360
  91.2 1.0 %copy.11 = f32[4,64,1024]{2,1,0:T(8,128)} copy(f32[4,64,1024]{2,1,0:T(8,128)S(1)} %shard_map.82) | data formatting | bytes 2097152
Async XLA Ops:
  0.9 1.6 %copy-start = (bf16[4,512,512]{2,1,0:T(8,128)(2,1)S(1)}, bf16[4,512,512]{2,1,0:T(8,128)(2,1)}, u32[]{:S(2)}) copy-start(bf16[4,512,512]{2,1,0:T(8,128)(2,1)} %constant.11.clone.wide_hbm) | copy-start | bytes 6291460
  2.5 0.9 %copy-start.1 = (f32[4,64,256]{2,1,0:T(8,128)S(1)}, f32[4,64,256]{2,1,0:T(8,128)}, u32[]{:S(2)}) copy-start(f32[4,64,256]{2,1,0:T(8,128)} %constant.10.clone.twist_hbm) | copy-start | bytes 786436
  3.5 0.8 copy-start.2
  4.3 0.8 copy-start.3
  5.1 0.8 copy-start.4
  5.9 0.7 copy-start.5
where the time goes:
time: 92.6 us; the launch traced here: 92.2 us
  Pallas kernels  84.6 us (91%)
  local copies, waits for them, and re-layouts  7.56 us (8%)
    pallas_call x1, Pallas kernels, body(): pl.pallas_call(kernel, out_shape=jax.ShapeDtypeStruct((TOK // SEQ, SEQ, C...  84.6 us
    unnamed x14, local copies, waits for them, and re-layouts  7.56 us

commit v1 on v0

--- a/solution.py
+++ b/solution.py
@@ -32,7 +32,7 @@
     m = np.arange(TOK)
     k2 = np.arange(TOK)
     column = np.arange(TOK)
-    m_of = 4 * (column % 64) + 2 * ((column // 64) % 2) + column // 128
+    m_of = 4 * (column // 64 % 2 * 32 + column % 32) + 2 * (column // 32 % 2) + column // 128
     coarse = 2 * np.pi * np.outer(k1 + 0.25, r) / SEQ
     head = np.concatenate([np.cos(coarse), -np.sin(coarse)], axis=0)
     head_high, head_low = split_parts(head)
@@ -67,15 +67,54 @@
 
 def kernel(
     streams_hbm, taps_hbm, gain_hbm, filter_hbm, head_hbm, tail_hbm, twist_hbm, wide_hbm,
-    out_ref,
+    out_hbm,
     stream, taps, gain, filt, head, tail, twist, wide,
-    rim_send, rim_recv, filt_send, filt_recv, filt_all, response,
-    gate_send, gate_recv, query_send, query_recv, conv_send, conv_recv,
-    load_sem, rim_sems, filt_sems, ring_sems, gate_out, gate_in, query_sems, conv_out, conv_in,
+    rim, filt_send, filt_recv, filt_all, response,
+    gate_send, gate_recv, near_send, near_recv, far_send, far_recv, conv_send, conv_recv, result,
+    load_sem, rim_sems, filt_sems, ring_sems, gate_out, gate_in, near_sems, far_sems,
+    conv_out, conv_in, out_sem,
 ):
     me = lax.axis_index("seq")
     group = lax.axis_index("grp")
+    plane, place, side = me // 8, lax.rem(me, 8), lax.rem(me, 2)
+    far_plane = lax.rem(plane + 2 + side, 8)
     barrier = pltpu.get_barrier_semaphore()
+
+    def load(source, target, slot):
+        return pltpu.make_async_copy(source, target, load_sem.at[slot])
+
+    def query_load(block):
+        lanes = pl.ds(block * LANES, LANES)
+        return load(streams_hbm.at[0, :, lanes], stream.at[0, block, pl.ds(8, TOK), :], block)
+
+    def gate_load(block):
+        lanes = pl.ds(block * LANES, LANES)
+        return load(
+            streams_hbm.at[pl.ds(1, 2), :, lanes],
+            stream.at[pl.ds(1, 2), block, pl.ds(8, TOK), :],
+            8 + block,
+        )
+
+    near_recv[...] = jnp.ones_like(near_recv)
+    for s in range(3):
+        stream[s, :, pl.ds(6, 2), :] = jnp.zeros((8, 2, LANES), jnp.float32)
+    small_loads = [
+        load(taps_hbm, taps, 16),
+        load(filter_hbm, filt, 17),
+        load(gain_hbm, gain, 18),
+        load(head_hbm, head, 19),
+        load(tail_hbm, tail, 20),
+        load(twist_hbm, twist, 21),
+        load(wide_hbm, wide, 22),
+    ]
+    small_loads[0].start()
+    for block in range(8):
+        query_load(block).start()
+    small_loads[1].start()
+    for block in range(8):
+        gate_load(block).start()
+    for copy in small_loads[2:]:
+        copy.start()
 
     def greet(step, carry):
         other = lax.rem(me + step, SEQ)
@@ -87,49 +126,75 @@
         pl.semaphore_signal(barrier, inc=1, device_id=(me, other), device_id_type=MESH)
         return carry
 
-    def load(source, target, slot):
-        return pltpu.make_async_copy(source, target, load_sem.at[slot])
-
-    def stream_load(block):
-        lanes = pl.ds(block * LANES, LANES)
-        return load(streams_hbm.at[:, :, lanes], stream.at[:, block, pl.ds(8, TOK), :], block)
-
-    for block in range(8):
-        stream_load(block).start()
-    small_loads = [
-        load(filter_hbm, filt, 8),
-        load(taps_hbm, taps, 9),
-        load(gain_hbm, gain, 10),
-        load(head_hbm, head, 11),
-        load(tail_hbm, tail, 12),
-        load(twist_hbm, twist, 13),
-        load(wide_hbm, wide, 14),
-    ]
-    for copy in small_loads:
-        copy.start()
     lax.fori_loop(1, SEQ, greet, 0)
     lax.fori_loop(1, GRP, greet_group, 0)
 
+    def wait_bytes(ref, sem):
+        pltpu.make_async_copy(ref, ref, sem).wait()
+
+    def feature(s, start, block, size, stride=None):
+        lanes = pl.ds(pl.multiple_of(block * LANES, LANES), LANES)
+
+        def rows(first):
+            window = pl.ds(first, size) if stride is None else pl.ds(first, size, stride)
+            return stream[s, block, window, :]
+
+        return (
+            taps[s, 0:1, lanes] * rows(start)
+            + taps[s, 1:2, lanes] * rows(start - 1)
+            + taps[s, 2:3, lanes] * rows(start - 2)
+        )
+
     small_loads[0].wait()
+    for block in range(8):
+        query_load(block).wait()
+
+    def near_query(block, carry):
+        for step in range(4):
+            goal = lax.rem(far_plane + 4 + step, 8)
+            for low in range(4):
+                featured = feature(0, 8 + goal * 32 + low, block, 8, 4)
+                near_send[pl.ds(goal * 256 + low * 8 + block, 8, 32), :] = featured
+        return carry
+
+    lax.fori_loop(0, 8, near_query, 0)
+    small_loads[1].wait()
     for half in range(2):
-        turned = jnp.transpose(filt[pl.ds(half * LANES, LANES), :])
-        filt_send[:, half, :] = turned
-    for block in range(8):
-        stream_load(block).wait()
-    rim_send[...] = jnp.zeros_like(rim_send)
-    for s in range(3):
-        rim_send[:, pl.ds(2 * s, 2), :] = stream[s, :, pl.ds(TOK + 6, 2), :]
+        filt_send[:, half, :] = filt[:, half * LANES : half * LANES + LANES]
+
     pl.semaphore_wait(barrier, SEQ - 1 + GRP - 1)
 
-    def rim_copy(other):
+    def rim_copy(block, other):
         return pltpu.make_async_remote_copy(
-            src_ref=rim_send, dst_ref=rim_recv, send_sem=rim_sems.at[0], recv_sem=rim_sems.at[1],
+            src_ref=streams_hbm.at[:, pl.ds(TOK - 8, 8), pl.ds(block * LANES, LANES)],
+            dst_ref=rim.at[:, block], send_sem=rim_sems.at[0], recv_sem=rim_sems.at[1],
             device_id=(other, group), device_id_type=MESH,
         )
 
     @pl.when(me < SEQ - 1)
     def _():
-        rim_copy(me + 1).start()
+        for block in range(8):
+            rim_copy(block, me + 1).start()
+
+    def near_copy(other):
+        return pltpu.make_async_remote_copy(
+            src_ref=near_send.at[pl.ds(pl.multiple_of(other * 32, 32), 32)],
+            dst_ref=near_recv.at[pl.ds(pl.multiple_of(me * 32, 32), 32)],
+            send_sem=near_sems.at[0], recv_sem=near_sems.at[1],
+            device_id=(other, group), device_id_type=MESH,
+        )
+
+    def send_near(step, carry):
+        goal = lax.rem(far_plane + 4 + lax.rem(step, 4), 8)
+        other = goal * 8 + lax.rem(place + step // 4, 8)
+
+        @pl.when((other != me) & (other != 0))
+        def _():
+            near_copy(other).start()
+
+        return carry
+
+    lax.fori_loop(0, 32, send_near, 0)
 
     def send_filter(step, carry):
         other = lax.rem(me + step, SEQ)
@@ -142,20 +207,8 @@
 
     lax.fori_loop(1, SEQ, send_filter, 0)
     filt_recv[me] = filt_send[me]
-    small_loads[1].wait()
-
-    def feature(s, start, block, size, stride=None):
-        lanes = pl.ds(pl.multiple_of(block * LANES, LANES), LANES)
-
-        def rows(first):
-            window = pl.ds(first, size) if stride is None else pl.ds(first, size, stride)
-            return stream[s, block, window, :]
-
-        return (
-            taps[s, 0:1, lanes] * rows(start)
-            + taps[s, 1:2, lanes] * rows(start - 1)
-            + taps[s, 2:3, lanes] * rows(start - 2)
-        )
+    for block in range(8):
+        gate_load(block).wait()
 
     def gate(quarter, half):
         for pair in range(2):
@@ -175,14 +228,9 @@
 
     @pl.when(me > 0)
     def _():
-        rim_copy(me).wait_recv()
+        wait_bytes(rim, rim_sems.at[1])
         for s in range(3):
-            stream[s, :, pl.ds(6, 2), :] = rim_recv[:, pl.ds(2 * s, 2), :]
-
-    @pl.when(me == 0)
-    def _():
-        for s in range(3):
-            stream[s, :, pl.ds(6, 2), :] = jnp.zeros((8, 2, LANES), jnp.float32)
+            stream[s, :, pl.ds(6, 2), :] = rim[s, :, pl.ds(6, 2), :]
 
     def gate_early(quarter, carry):
         gate(quarter, 0)
@@ -202,32 +250,47 @@
         gate_recv[quarter, own, :] = gate_send[quarter, own, :]
         return carry
 
-    lax.fori_loop(0, QUARTERS, gate_early, 0)
-
-    def query(block, carry):
-        for low in range(4):
-            featured = feature(0, 8 + low, block, SEQ, 4)
-            query_send[pl.ds(low * 8 + block, SEQ, 32), :] = featured
-        return carry
-
-    lax.fori_loop(0, 8, query, 0)
-
-    def send_query(step, carry):
+    gate_early(0, 0)
+
+    for low in range(2):
+        for block in range(8):
+            near_send[pl.ds(low * 8 + block, 1), :] = feature(0, 8 + low, block, 1)
+
+    @pl.when((me != 0) & (far_plane != 0) & (far_plane < 5))
+    def _():
+        near_copy(0).start()
+
+    own_near = pl.ds(pl.multiple_of(me * 32, 32), 32)
+    near_recv[own_near, :] = near_send[own_near, :]
+
+    def far_query(block, carry):
+        pieces = []
+        for low in (0, 2, 1, 3):
+            for residue in range(4):
+                goal = lax.rem(far_plane + lax.rem(residue - far_plane + 8, 4), 8)
+                pieces.append(feature(0, 8 + goal * 32 + low, block, 8, 4))
+        turned = jnp.transpose(jnp.concatenate(pieces, axis=0))
+        for own in range(2):
+            far_send[pl.ds(block * 2 + own, SEQ, 16), :] = turned[own * 64 : own * 64 + 64]
+        return carry
+
+    lax.fori_loop(0, 8, far_query, 0)
+
+    def send_far(step, carry):
         other = lax.rem(me + step, SEQ)
         pltpu.make_async_remote_copy(
-            src_ref=query_send.at[pl.ds(pl.multiple_of(other * 32, 32), 32)],
-            dst_ref=query_recv.at[pl.ds(pl.multiple_of(me * 32, 32), 32)],
-            send_sem=query_sems.at[0], recv_sem=query_sems.at[1],
+            src_ref=far_send.at[pl.ds(pl.multiple_of(other * 16, 16), 16)],
+            dst_ref=far_recv.at[pl.ds(pl.multiple_of(me * 16, 16), 16)],
+            send_sem=far_sems.at[0], recv_sem=far_sems.at[1],
             device_id=(other, group), device_id_type=MESH,
         ).start()
         return carry
 
-    lax.fori_loop(1, SEQ, send_query, 0)
-    own_query = pl.ds(pl.multiple_of(me * 32, 32), 32)
-    query_recv[own_query, :] = query_send[own_query, :]
-
-    def wait_bytes(ref, sem):
-        pltpu.make_async_copy(ref, ref, sem).wait()
+    lax.fori_loop(1, SEQ, send_far, 0)
+    own_far = pl.ds(pl.multiple_of(me * 16, 16), 16)
+    far_recv[own_far, :] = far_send[own_far, :]
+
+    lax.fori_loop(1, QUARTERS, gate_early, 0)
 
     wait_bytes(filt_recv.at[pl.ds(0, SEQ - 1)], filt_sems.at[1])
     for half in range(2):
@@ -262,6 +325,14 @@
 
     wait_bytes(filt_all.at[pl.ds(0, GRP - 1)], ring_sems.at[1])
     response[...] = spectrum(lambda f: filt_all[f])
+
+    token = lax.broadcasted_iota(jnp.int32, (SEQ, LANES), 0)
+    lane = lax.broadcasted_iota(jnp.int32, (SEQ, LANES), 1)
+    goal_plane = lane // 64 * 4 + lane % 32 // 8
+    is_far = (goal_plane - token // 8 - 2 - token % 2 + 16) % 8 < 4
+    is_low = lane < 64
+
+    wait_bytes(far_recv.at[pl.ds(0, (SEQ - 1) * 16)], far_sems.at[1])
 
     def convolve(quarter, carry):
         wait_bytes(gate_recv.at[quarter, pl.ds(0, (SEQ - 1) * 8)], gate_in.at[quarter])
@@ -294,13 +365,18 @@
                 [real * twist[2] - imag * twist[3], real * twist[3] + imag * twist[2]], axis=0
             )
             high, low = halves(turned)
-            result = product(tail[...], jnp.concatenate([high, low, high], axis=0))
-            stacked = jnp.concatenate([result[:, :LANES], result[:, LANES:]], axis=0)
+            summed = product(tail[...], jnp.concatenate([high, low, high], axis=0))
+            asked = far_recv[pl.ds(quarter * 4 + f, SEQ, 16), :]
+            swapped = pltpu.roll(asked, 64, 1)
+            first = jnp.where(is_far, jnp.where(is_low, asked, swapped), 1.0)
+            second = jnp.where(is_far, jnp.where(is_low, swapped, asked), 1.0)
+            stacked = jnp.concatenate(
+                [summed[:, :LANES] * first, summed[:, LANES:] * second], axis=0
+            )
             flipped = jnp.transpose(stacked)
-            for upper in range(2):
-                conv_send[quarter, pl.ds(upper * 4 + f, SEQ, 8), :] = flipped[
-                    upper * 64 : upper * 64 + 64
-                ]
+            for part in range(4):
+                start = part // 2 * 256 + part % 2 * 4 + f
+                conv_send[quarter, pl.ds(start, 32, 8), :] = flipped[part * 32 : part * 32 + 32]
 
         def send(step, inner):
             other = lax.rem(me + step, SEQ)
@@ -319,7 +395,13 @@
 
     lax.fori_loop(0, QUARTERS, convolve, 0)
 
-    wait_bytes(query_recv.at[pl.ds(0, (SEQ - 1) * 32)], query_sems.at[1])
+    wait_bytes(near_recv.at[pl.ds(0, 31 * 32)], near_sems.at[1])
+
+    def store(quarter):
+        lanes = pl.ds(pl.multiple_of(quarter * 256, 256), 256)
+        return pltpu.make_async_copy(
+            result.at[:, :, lanes], out_hbm.at[:, :, lanes], out_sem.at[quarter]
+        )
 
     def finish(quarter, carry):
         wait_bytes(conv_recv.at[quarter, pl.ds(0, (SEQ - 1) * 8)], conv_in.at[quarter])
@@ -331,48 +413,50 @@
                     [conv_recv[quarter, pl.ds(upper * 4 + pair * 2 + own, SEQ, 8), :] for own in range(2)],
                     axis=0,
                 )
-                result = jnp.transpose(gathered)
+                turned = jnp.transpose(gathered)
                 for lower in range(2):
                     offset = upper * 2 + lower
-                    asked = query_recv[pl.ds(offset * 8 + block, SEQ, 32), :]
-                    out_ref[offset, :, lanes] = asked * result[lower * 64 : lower * 64 + 64]
+                    asked = near_recv[pl.ds(offset * 8 + block, SEQ, 32), :]
+                    result[offset, :, lanes] = asked * turned[lower * 64 : lower * 64 + 64]
+        store(quarter).start()
         return carry
 
     lax.fori_loop(0, QUARTERS, finish, 0)
 
     @pl.when(me < SEQ - 1)
     def _():
-        rim_copy(me + 1).wait_send()
+        wait_bytes(streams_hbm.at[:, pl.ds(TOK - 8, 8), :], rim_sems.at[0])
 
     wait_bytes(filt_send.at[pl.ds(0, SEQ - 1)], filt_sems.at[0])
     wait_bytes(filt_all.at[pl.ds(0, GRP - 1)], ring_sems.at[0])
-    wait_bytes(query_send.at[pl.ds(0, (SEQ - 1) * 32)], query_sems.at[0])
+    wait_bytes(near_send.at[pl.ds(0, 31 * 32)], near_sems.at[0])
+    wait_bytes(far_send.at[pl.ds(0, (SEQ - 1) * 16)], far_sems.at[0])
     for quarter in range(QUARTERS):
         wait_bytes(gate_send.at[quarter, pl.ds(0, (SEQ - 1) * 8)], gate_out.at[quarter])
         wait_bytes(conv_send.at[quarter, pl.ds(0, (SEQ - 1) * 8)], conv_out.at[quarter])
+        store(quarter).wait()
 
 
 def body(streams, short_filters, skip_gain, long_filter):
     head_all, tail_all, twists, wide = tables()
     dma = pltpu.SemaphoreType.DMA
     f32 = jnp.float32
-    any_space = pl.BlockSpec(memory_space=pl.ANY)
+    in_hbm = pl.BlockSpec(memory_space=pltpu.HBM)
     return pl.pallas_call(
         kernel,
         out_shape=jax.ShapeDtypeStruct((TOK // SEQ, SEQ, CH), f32),
-        in_specs=[any_space] * 8,
-        out_specs=pl.BlockSpec(memory_space=pltpu.VMEM),
+        in_specs=[in_hbm] * 8,
+        out_specs=in_hbm,
         scratch_shapes=[
             pltpu.VMEM((3, 8, TOK + 8, LANES), f32),
             pltpu.VMEM((3, 3, CH), f32),
             pltpu.SMEM((CH,), f32),
-            pltpu.VMEM((TOK, 64), f32),
+            pltpu.VMEM((64, TOK), f32),
             pltpu.VMEM(head_all.shape, jnp.bfloat16),
             pltpu.VMEM(tail_all.shape, jnp.bfloat16),
             pltpu.VMEM(twists.shape, f32),
             pltpu.VMEM(wide.shape, jnp.bfloat16),
-            pltpu.VMEM((8, 8, LANES), f32),
-            pltpu.VMEM((8, 8, LANES), f32),
+            pltpu.VMEM((3, 8, 8, LANES), f32),
             pltpu.VMEM((SEQ, 2, LANES), f32),
             pltpu.VMEM((SEQ, 2, LANES), f32),
             pltpu.VMEM((GRP, SEQ, TOK), f32),
@@ -381,22 +465,27 @@
             pltpu.VMEM((QUARTERS, SEQ * 8, LANES), f32),
             pltpu.VMEM((SEQ * 32, LANES), f32),
             pltpu.VMEM((SEQ * 32, LANES), f32),
+            pltpu.VMEM((SEQ * 16, LANES), f32),
+            pltpu.VMEM((SEQ * 16, LANES), f32),
             pltpu.VMEM((QUARTERS, SEQ * 8, LANES), f32),
             pltpu.VMEM((QUARTERS, SEQ * 8, LANES), f32),
-            dma((15,)),
+            pltpu.VMEM((TOK // SEQ, SEQ, CH), f32),
+            dma((23,)),
             dma((2,)),
             dma((2,)),
             dma((2,)),
             dma((QUARTERS,)),
             dma((QUARTERS,)),
             dma((2,)),
+            dma((2,)),
+            dma((QUARTERS,)),
             dma((QUARTERS,)),
             dma((QUARTERS,)),
         ],
         compiler_params=pltpu.CompilerParams(
-            collective_id=0, has_side_effects=True, vmem_limit_bytes=48 << 20
+            collective_id=0, has_side_effects=True, vmem_limit_bytes=60 << 20
         ),
-    )(streams, short_filters, skip_gain, long_filter, head_all, tail_all, twists, wide)
+    )(streams, short_filters, skip_gain, long_filter.T, head_all, tail_all, twists, wide)
 
 
 def solution(mesh):

time: 92.6 us -> 81.3 us (0.88)
  Pallas kernels: 84.6 us -> 78.9 us
  local copies, waits for them, and re-layouts: 7.56 us -> 2.31 us
    pallas_call x1, Pallas kernels: 84.6 us -> 78.9 us  [body(): pl.pallas_call(kernel, out_shape=jax.ShapeDtypeStruct((TOK // SEQ, SEQ, C...]
    unnamed x14 -> x1, local copies, waits for them, and re-layouts: 7.56 us -> 2.31 us
where the time goes in v1:
time: 81.3 us; the launch traced here: 81.2 us
  Pallas kernels  78.9 us (97%)
  local copies, waits for them, and re-layouts  2.31 us (3%)
    pallas_call x1, Pallas kernels, body(): pl.pallas_call(kernel, out_shape=jax.ShapeDtypeStruct((TOK // SEQ, SEQ, C...  78.9 us
    unnamed x1, local copies, waits for them, and re-layouts  2.31 us

profile of v1, /device:TPU:1, one launch (start us, length us, event | category | flops | bytes accessed | tf_op | source)
XLA Modules:
  0.0 81.2 jit_solution(18444146022216429754)
XLA Ops:
  0.0 78.9 %shard_map.82 = f32[4,64,1024]{2,1,0:T(8,128)} custom-call(f32[3,256,1024]{2,1,0:T(8,128)} %streams_hbm.1, f32[3,3,1024]{2,1,0:T(4,128)} %taps_hbm.1, f32[1024]{0:T(1024)} %gain_hbm.1, f32[64,256]{1,0:T(8,128)} %bitcast.1, bf16[128,192]{1,0:T(8,128)(2,1)} %constant.8.clone.head_hbm, bf16[64,384]{1,0:T(8,128)(2,1)} %constant.9.clone.tail_hbm, ...), custom_call_target="tpu_custom_call" | custom-call | tf_op jit(solution)/shard_map/pallas_call | solution.py:445
  78.9 2.3 %copy.10 = f32[4,64,1024]{2,1,0:T(8,128)} copy(f32[4,64,1024]{2,1,0:T(8,128)} %shard_map.82) | data formatting | bytes 2097152

commit v2 on v1

--- a/solution.py
+++ b/solution.py
@@ -67,12 +67,12 @@
 
 def kernel(
     streams_hbm, taps_hbm, gain_hbm, filter_hbm, head_hbm, tail_hbm, twist_hbm, wide_hbm,
-    out_hbm,
+    out_ref,
     stream, taps, gain, filt, head, tail, twist, wide,
     rim, filt_send, filt_recv, filt_all, response,
-    gate_send, gate_recv, near_send, near_recv, far_send, far_recv, conv_send, conv_recv, result,
+    gate_send, gate_recv, near_send, near_recv, far_send, far_recv, conv_send, conv_recv,
     load_sem, rim_sems, filt_sems, ring_sems, gate_out, gate_in, near_sems, far_sems,
-    conv_out, conv_in, out_sem,
+    conv_out, conv_in,
 ):
     me = lax.axis_index("seq")
     group = lax.axis_index("grp")
@@ -95,9 +95,6 @@
             8 + block,
         )
 
-    near_recv[...] = jnp.ones_like(near_recv)
-    for s in range(3):
-        stream[s, :, pl.ds(6, 2), :] = jnp.zeros((8, 2, LANES), jnp.float32)
     small_loads = [
         load(taps_hbm, taps, 16),
         load(filter_hbm, filt, 17),
@@ -110,24 +107,26 @@
     small_loads[0].start()
     for block in range(8):
         query_load(block).start()
+
+    def greet(step, carry):
+        other = lax.rem(me + step, SEQ)
+        pl.semaphore_signal(barrier, inc=1, device_id=(other, group), device_id_type=MESH)
+        return carry
+
+    def greet_group(step, carry):
+        other = lax.rem(group + step, GRP)
+        pl.semaphore_signal(barrier, inc=1, device_id=(me, other), device_id_type=MESH)
+        return carry
+
+    lax.fori_loop(1, SEQ, greet, 0)
+    lax.fori_loop(1, GRP, greet_group, 0)
     small_loads[1].start()
     for block in range(8):
         gate_load(block).start()
     for copy in small_loads[2:]:
         copy.start()
-
-    def greet(step, carry):
-        other = lax.rem(me + step, SEQ)
-        pl.semaphore_signal(barrier, inc=1, device_id=(other, group), device_id_type=MESH)
-        return carry
-
-    def greet_group(step, carry):
-        other = lax.rem(group + step, GRP)
-        pl.semaphore_signal(barrier, inc=1, device_id=(me, other), device_id_type=MESH)
-        return carry
-
-    lax.fori_loop(1, SEQ, greet, 0)
-    lax.fori_loop(1, GRP, greet_group, 0)
+    for s in range(3):
+        stream[s, :, pl.ds(6, 2), :] = jnp.zeros((8, 2, LANES), jnp.float32)
 
     def wait_bytes(ref, sem):
         pltpu.make_async_copy(ref, ref, sem).wait()
@@ -396,12 +395,16 @@
     lax.fori_loop(0, QUARTERS, convolve, 0)
 
     wait_bytes(near_recv.at[pl.ds(0, 31 * 32)], near_sems.at[1])
-
-    def store(quarter):
-        lanes = pl.ds(pl.multiple_of(quarter * 256, 256), 256)
-        return pltpu.make_async_copy(
-            result.at[:, :, lanes], out_hbm.at[:, :, lanes], out_sem.at[quarter]
-        )
+    came = (plane - token // 8 - 2 - token % 2 + 16) % 8 >= 4
+
+    def stage(block, carry):
+        lanes = pl.ds(pl.multiple_of(block * LANES, LANES), LANES)
+        for offset in range(4):
+            asked = near_recv[pl.ds(offset * 8 + block, SEQ, 32), :]
+            out_ref[offset, :, lanes] = jnp.where(came, asked, 1.0)
+        return carry
+
+    lax.fori_loop(0, 8, stage, 0)
 
     def finish(quarter, carry):
         wait_bytes(conv_recv.at[quarter, pl.ds(0, (SEQ - 1) * 8)], conv_in.at[quarter])
@@ -416,9 +419,8 @@
                 turned = jnp.transpose(gathered)
                 for lower in range(2):
                     offset = upper * 2 + lower
-                    asked = near_recv[pl.ds(offset * 8 + block, SEQ, 32), :]
-                    result[offset, :, lanes] = asked * turned[lower * 64 : lower * 64 + 64]
-        store(quarter).start()
+                    asked = out_ref[offset, :, lanes]
+                    out_ref[offset, :, lanes] = asked * turned[lower * 64 : lower * 64 + 64]
         return carry
 
     lax.fori_loop(0, QUARTERS, finish, 0)
@@ -434,7 +436,6 @@
     for quarter in range(QUARTERS):
         wait_bytes(gate_send.at[quarter, pl.ds(0, (SEQ - 1) * 8)], gate_out.at[quarter])
         wait_bytes(conv_send.at[quarter, pl.ds(0, (SEQ - 1) * 8)], conv_out.at[quarter])
-        store(quarter).wait()
 
 
 def body(streams, short_filters, skip_gain, long_filter):
@@ -446,7 +447,7 @@
         kernel,
         out_shape=jax.ShapeDtypeStruct((TOK // SEQ, SEQ, CH), f32),
         in_specs=[in_hbm] * 8,
-        out_specs=in_hbm,
+        out_specs=pl.BlockSpec(memory_space=pltpu.VMEM),
         scratch_shapes=[
             pltpu.VMEM((3, 8, TOK + 8, LANES), f32),
             pltpu.VMEM((3, 3, CH), f32),
@@ -469,7 +470,6 @@
             pltpu.VMEM((SEQ * 16, LANES), f32),
             pltpu.VMEM((QUARTERS, SEQ * 8, LANES), f32),
             pltpu.VMEM((QUARTERS, SEQ * 8, LANES), f32),
-            pltpu.VMEM((TOK // SEQ, SEQ, CH), f32),
             dma((23,)),
             dma((2,)),
             dma((2,)),
@@ -480,12 +480,11 @@
             dma((2,)),
             dma((QUARTERS,)),
             dma((QUARTERS,)),
-            dma((QUARTERS,)),
         ],
         compiler_params=pltpu.CompilerParams(
-            collective_id=0, has_side_effects=True, vmem_limit_bytes=60 << 20
+            collective_id=0, has_side_effects=True, vmem_limit_bytes=48 << 20
         ),
-    )(streams, short_filters, skip_gain, long_filter.T, head_all, tail_all, twists, wide)
+    )(*[pltpu.with_memory_space_constraint(x, pltpu.HBM) for x in (streams, short_filters, skip_gain, long_filter.T, jnp.asarray(head_all), jnp.asarray(tail_all), jnp.asarray(twists), jnp.asarray(wide))])
 
 
 def solution(mesh):

time: 81.3 us -> 79.1 us (0.973)
  local copies, waits for them, and re-layouts: 2.31 us -> 0.97 us
  Pallas kernels: 78.9 us -> 78 us
    unnamed x1, local copies, waits for them, and re-layouts: 2.31 us -> 0.97 us
    pallas_call x1, Pallas kernels: 78.9 us -> 78 us  [body(): pl.pallas_call(kernel, out_shape=jax.ShapeDtypeStruct((TOK // SEQ, SEQ, C...]
where the time goes in v2:
time: 79.1 us; the launch traced here: 79 us
  Pallas kernels  78 us (99%)
  local copies, waits for them, and re-layouts  0.97 us (1%)
    pallas_call x1, Pallas kernels, body(): pl.pallas_call(kernel, out_shape=jax.ShapeDtypeStruct((TOK // SEQ, SEQ, C...  78 us

profile of v2, /device:TPU:1, one launch (start us, length us, event | category | flops | bytes accessed | tf_op | source)
XLA Modules:
  0.0 79.0 jit_solution(5191504711241610272)
XLA Ops:
  0.0 78.0 %shard_map.82 = f32[4,64,1024]{2,1,0:T(8,128)S(1)} custom-call(f32[3,256,1024]{2,1,0:T(8,128)} %streams_hbm.1, f32[3,3,1024]{2,1,0:T(4,128)} %taps_hbm.1, f32[1024]{0:T(1024)} %gain_hbm.1, f32[64,256]{1,0:T(8,128)} %bitcast.1, bf16[128,192]{1,0:T(8,128)(2,1)} %constant.8.clone.head_hbm, bf16[64,384]{1,0:T(8,128)(2,1)} %constant.9.clone.tail_hbm, ...), custom_call_target="tpu_custom_call" | custom-call | tf_op jit(solution)/shard_map/pallas_call | solution.py:446
  78.0 1.0 %copy.10 = f32[4,64,1024]{2,1,0:T(8,128)} copy(f32[4,64,1024]{2,1,0:T(8,128)S(1)} %shard_map.82) | data formatting | bytes 2097152

commit v3 on v2

--- a/solution.py
+++ b/solution.py
@@ -70,14 +70,16 @@
     out_ref,
     stream, taps, gain, filt, head, tail, twist, wide,
     rim, filt_send, filt_recv, filt_all, response,
-    gate_send, gate_recv, near_send, near_recv, far_send, far_recv, conv_send, conv_recv,
-    load_sem, rim_sems, filt_sems, ring_sems, gate_out, gate_in, near_sems, far_sems,
+    gate_send, gate_recv, near_send, near_recv, far_send, far_recv, anti_send, anti_recv,
+    own_send, own_recv, conv_send, conv_recv,
+    load_sem, rim_sems, filt_sems, ring_sems, gate_out, gate_in, near_sems, far_sems, anti_sems, own_sems,
     conv_out, conv_in,
 ):
     me = lax.axis_index("seq")
     group = lax.axis_index("grp")
     plane, place, side = me // 8, lax.rem(me, 8), lax.rem(me, 2)
     far_plane = lax.rem(plane + 2 + side, 8)
+    opposite = lax.rem(plane + 4, 8)
     barrier = pltpu.get_barrier_semaphore()
 
     def load(source, target, slot):
@@ -148,15 +150,23 @@
     for block in range(8):
         query_load(block).wait()
 
-    def near_query(block, carry):
-        for step in range(4):
-            goal = lax.rem(far_plane + 4 + step, 8)
-            for low in range(4):
-                featured = feature(0, 8 + goal * 32 + low, block, 8, 4)
-                near_send[pl.ds(goal * 256 + low * 8 + block, 8, 32), :] = featured
-        return carry
-
-    lax.fori_loop(0, 8, near_query, 0)
+    def packed_query(start, size, stride, low, rows):
+        owned = lax.broadcasted_iota(jnp.int32, (size, LANES), 1) % 64 // 8 == plane
+        last = feature(0, start, 7, size, stride)
+        for block in range(7):
+            shift = lax.rem(plane - lax.rem(plane + 1 + block, 8) + 16, 16) * 8
+            moved = pltpu.roll(last, shift, 1)
+            near_send[rows, block, low, :] = jnp.where(
+                owned, moved, feature(0, start, block, size, stride)
+            )
+
+    def near_query(step, carry):
+        goal = lax.rem(far_plane + 4 + step, 8)
+        for low in range(4):
+            packed_query(8 + goal * 32 + low, 8, 4, low, pl.ds(goal * 8, 8))
+        return carry
+
+    lax.fori_loop(0, 4, near_query, 0)
     small_loads[1].wait()
     for half in range(2):
         filt_send[:, half, :] = filt[:, half * LANES : half * LANES + LANES]
@@ -177,8 +187,7 @@
 
     def near_copy(other):
         return pltpu.make_async_remote_copy(
-            src_ref=near_send.at[pl.ds(pl.multiple_of(other * 32, 32), 32)],
-            dst_ref=near_recv.at[pl.ds(pl.multiple_of(me * 32, 32), 32)],
+            src_ref=near_send.at[other], dst_ref=near_recv.at[me],
             send_sem=near_sems.at[0], recv_sem=near_sems.at[1],
             device_id=(other, group), device_id_type=MESH,
         )
@@ -252,44 +261,86 @@
     gate_early(0, 0)
 
     for low in range(2):
-        for block in range(8):
-            near_send[pl.ds(low * 8 + block, 1), :] = feature(0, 8 + low, block, 1)
+        packed_query(8 + low, 1, None, low, pl.ds(0, 1))
 
     @pl.when((me != 0) & (far_plane != 0) & (far_plane < 5))
     def _():
         near_copy(0).start()
 
-    own_near = pl.ds(pl.multiple_of(me * 32, 32), 32)
-    near_recv[own_near, :] = near_send[own_near, :]
-
-    def far_query(block, carry):
+    near_recv[me] = near_send[me]
+
+    def turned_query(block, first, target):
         pieces = []
         for low in (0, 2, 1, 3):
             for residue in range(4):
-                goal = lax.rem(far_plane + lax.rem(residue - far_plane + 8, 4), 8)
+                goal = lax.rem(first + lax.rem(residue - far_plane + 8, 4), 8)
                 pieces.append(feature(0, 8 + goal * 32 + low, block, 8, 4))
         turned = jnp.transpose(jnp.concatenate(pieces, axis=0))
         for own in range(2):
-            far_send[pl.ds(block * 2 + own, SEQ, 16), :] = turned[own * 64 : own * 64 + 64]
+            target[pl.ds(block * 2 + own, SEQ, 16), :] = turned[own * 64 : own * 64 + 64]
+
+    def far_query(block, carry):
+        turned_query(block, far_plane, far_send)
         return carry
 
     lax.fori_loop(0, 8, far_query, 0)
 
     def send_far(step, carry):
         other = lax.rem(me + step, SEQ)
-        pltpu.make_async_remote_copy(
-            src_ref=far_send.at[pl.ds(pl.multiple_of(other * 16, 16), 16)],
-            dst_ref=far_recv.at[pl.ds(pl.multiple_of(me * 16, 16), 16)],
-            send_sem=far_sems.at[0], recv_sem=far_sems.at[1],
-            device_id=(other, group), device_id_type=MESH,
-        ).start()
+
+        @pl.when(other // 8 != opposite)
+        def _():
+            pltpu.make_async_remote_copy(
+                src_ref=far_send.at[pl.ds(pl.multiple_of(other * 16, 16), 16)],
+                dst_ref=far_recv.at[pl.ds(pl.multiple_of(me * 16, 16), 16)],
+                send_sem=far_sems.at[0], recv_sem=far_sems.at[1],
+                device_id=(other, group), device_id_type=MESH,
+            ).start()
+
         return carry
 
     lax.fori_loop(1, SEQ, send_far, 0)
     own_far = pl.ds(pl.multiple_of(me * 16, 16), 16)
     far_recv[own_far, :] = far_send[own_far, :]
 
+    slab = [far_send[pl.ds(opposite * 128 + i, 8, 16), :] for i in range(16)]
+    turned = jnp.transpose(jnp.concatenate(slab, axis=0))
+    for low in range(4):
+        anti_send[:, low, :] = turned[low * 32 : low * 32 + 32]
+
+    def send_anti(step, carry):
+        residue = lax.rem(step, 4)
+        goal = lax.rem(far_plane + lax.rem(residue - far_plane + 8, 4), 8)
+        spot = lax.rem(place + step // 4, 8)
+        pltpu.make_async_remote_copy(
+            src_ref=anti_send.at[residue * 8 + spot], dst_ref=anti_recv.at[me],
+            send_sem=anti_sems.at[0], recv_sem=anti_sems.at[1],
+            device_id=(goal * 8 + spot, group), device_id_type=MESH,
+        ).start()
+        return carry
+
+    lax.fori_loop(0, 32, send_anti, 0)
+
     lax.fori_loop(1, QUARTERS, gate_early, 0)
+
+    def own_query(block, carry):
+        turned_query(block, far_plane + 4, own_send)
+        return carry
+
+    lax.fori_loop(0, 8, own_query, 0)
+
+    def send_own(step, carry):
+        other = plane * 8 + lax.rem(place + step, 8)
+        pltpu.make_async_remote_copy(
+            src_ref=own_send.at[pl.ds(pl.multiple_of(other * 16, 16), 16)],
+            dst_ref=own_recv.at[pl.ds(pl.multiple_of(me * 16, 16), 16)],
+            send_sem=own_sems.at[0], recv_sem=own_sems.at[1],
+            device_id=(other, group), device_id_type=MESH,
+        ).start()
+        return carry
+
+    lax.fori_loop(1, 8, send_own, 0)
+    own_recv[own_far, :] = own_send[own_far, :]
 
     wait_bytes(filt_recv.at[pl.ds(0, SEQ - 1)], filt_sems.at[1])
     for half in range(2):
@@ -329,9 +380,12 @@
     lane = lax.broadcasted_iota(jnp.int32, (SEQ, LANES), 1)
     goal_plane = lane // 64 * 4 + lane % 32 // 8
     is_far = (goal_plane - token // 8 - 2 - token % 2 + 16) % 8 < 4
+    is_own = jnp.logical_not(is_far) & (token // 8 == plane)
+    is_far = is_far & ((token // 8 - plane + 8) % 8 != 4)
     is_low = lane < 64
 
-    wait_bytes(far_recv.at[pl.ds(0, (SEQ - 1) * 16)], far_sems.at[1])
+    wait_bytes(far_recv.at[pl.ds(0, (SEQ - 9) * 16)], far_sems.at[1])
+    wait_bytes(own_recv.at[pl.ds(0, 7 * 16)], own_sems.at[1])
 
     def convolve(quarter, carry):
         wait_bytes(gate_recv.at[quarter, pl.ds(0, (SEQ - 1) * 8)], gate_in.at[quarter])
@@ -367,8 +421,12 @@
             summed = product(tail[...], jnp.concatenate([high, low, high], axis=0))
             asked = far_recv[pl.ds(quarter * 4 + f, SEQ, 16), :]
             swapped = pltpu.roll(asked, 64, 1)
-            first = jnp.where(is_far, jnp.where(is_low, asked, swapped), 1.0)
-            second = jnp.where(is_far, jnp.where(is_low, swapped, asked), 1.0)
+            mine = own_recv[pl.ds(quarter * 4 + f, SEQ, 16), :]
+            crossed_mine = pltpu.roll(mine, 64, 1)
+            first = jnp.where(is_own, jnp.where(is_low, mine, crossed_mine), 1.0)
+            second = jnp.where(is_own, jnp.where(is_low, crossed_mine, mine), 1.0)
+            first = jnp.where(is_far, jnp.where(is_low, asked, swapped), first)
+            second = jnp.where(is_far, jnp.where(is_low, swapped, asked), second)
             stacked = jnp.concatenate(
                 [summed[:, :LANES] * first, summed[:, LANES:] * second], axis=0
             )
@@ -394,17 +452,48 @@
 
     lax.fori_loop(0, QUARTERS, convolve, 0)
 
-    wait_bytes(near_recv.at[pl.ds(0, 31 * 32)], near_sems.at[1])
+    wait_bytes(near_recv.at[pl.ds(0, 31)], near_sems.at[1])
     came = (plane - token // 8 - 2 - token % 2 + 16) % 8 >= 4
+    wait_bytes(anti_recv.at[pl.ds(0, 32)], anti_sems.at[1])
+    crossed = lane % 64 // 8 == (token // 8 + 4) % 8
+
+    lane_plane = lane % 64 // 8
+    apart = lane_plane != token // 8
+
+    def far_factor(block, offset):
+        packed = anti_recv[:, offset % 2 * 2 + offset // 2, :]
+        firsts, seconds = [], []
+        for z in range(8):
+            rows = packed[z * 8 : z * 8 + 8]
+            shift = (z + 4) % 8 * 8 + 128 - 16 * block
+            firsts.append(pltpu.roll(rows, lax.rem(shift, LANES), 1))
+            seconds.append(pltpu.roll(rows, lax.rem(shift + 56, LANES), 1))
+        opened = jnp.where(
+            is_low, jnp.concatenate(firsts, axis=0), jnp.concatenate(seconds, axis=0)
+        )
+        return jnp.where(crossed, opened, 1.0)
 
     def stage(block, carry):
         lanes = pl.ds(pl.multiple_of(block * LANES, LANES), LANES)
         for offset in range(4):
-            asked = near_recv[pl.ds(offset * 8 + block, SEQ, 32), :]
-            out_ref[offset, :, lanes] = jnp.where(came, asked, 1.0)
-        return carry
-
-    lax.fori_loop(0, 8, stage, 0)
+            asked = jnp.where(apart, near_recv[:, block, offset, :], 1.0)
+            out_ref[offset, :, lanes] = jnp.where(came, asked, far_factor(block, offset))
+        return carry
+
+    lax.fori_loop(0, 7, stage, 0)
+    for offset in range(4):
+        gathered = jnp.ones((SEQ, LANES), jnp.float32)
+        for block in range(7):
+            source = near_recv[:, block, offset, :]
+            pieces = []
+            for z in range(8):
+                shift = ((z + 1 + block) % 8 - z) * 8 % LANES
+                pieces.append(pltpu.roll(source[z * 8 : z * 8 + 8], shift, 1))
+            here = lane_plane == (token // 8 + 1 + block) % 8
+            gathered = jnp.where(here, jnp.concatenate(pieces, axis=0), gathered)
+        out_ref[offset, :, pl.ds(7 * LANES, LANES)] = jnp.where(
+            came, gathered, far_factor(7, offset)
+        )
 
     def finish(quarter, carry):
         wait_bytes(conv_recv.at[quarter, pl.ds(0, (SEQ - 1) * 8)], conv_in.at[quarter])
@@ -431,8 +520,10 @@
 
     wait_bytes(filt_send.at[pl.ds(0, SEQ - 1)], filt_sems.at[0])
     wait_bytes(filt_all.at[pl.ds(0, GRP - 1)], ring_sems.at[0])
-    wait_bytes(near_send.at[pl.ds(0, 31 * 32)], near_sems.at[0])
-    wait_bytes(far_send.at[pl.ds(0, (SEQ - 1) * 16)], far_sems.at[0])
+    wait_bytes(near_send.at[pl.ds(0, 31)], near_sems.at[0])
+    wait_bytes(own_send.at[pl.ds(0, 7 * 16)], own_sems.at[0])
+    wait_bytes(far_send.at[pl.ds(0, (SEQ - 9) * 16)], far_sems.at[0])
+    wait_bytes(anti_send, anti_sems.at[0])
     for quarter in range(QUARTERS):
         wait_bytes(gate_send.at[quarter, pl.ds(0, (SEQ - 1) * 8)], gate_out.at[quarter])
         wait_bytes(conv_send.at[quarter, pl.ds(0, (SEQ - 1) * 8)], conv_out.at[quarter])
@@ -464,8 +555,12 @@
             pltpu.VMEM((TOK, 2 * TOK), f32),
             pltpu.VMEM((QUARTERS, SEQ * 8, LANES), f32),
             pltpu.VMEM((QUARTERS, SEQ * 8, LANES), f32),
-            pltpu.VMEM((SEQ * 32, LANES), f32),
-            pltpu.VMEM((SEQ * 32, LANES), f32),
+            pltpu.VMEM((SEQ, 7, 4, LANES), f32),
+            pltpu.VMEM((SEQ, 7, 4, LANES), f32),
+            pltpu.VMEM((SEQ * 16, LANES), f32),
+            pltpu.VMEM((SEQ * 16, LANES), f32),
+            pltpu.VMEM((32, 4, LANES), f32),
+            pltpu.VMEM((SEQ, 4, LANES), f32),
             pltpu.VMEM((SEQ * 16, LANES), f32),
             pltpu.VMEM((SEQ * 16, LANES), f32),
             pltpu.VMEM((QUARTERS, SEQ * 8, LANES), f32),
@@ -476,6 +571,8 @@
             dma((2,)),
             dma((QUARTERS,)),
             dma((QUARTERS,)),
+            dma((2,)),
+            dma((2,)),
             dma((2,)),
             dma((2,)),
             dma((QUARTERS,)),

time: 79.1 us -> 77.9 us (0.985)
  Pallas kernels: 78 us -> 76.8 us
    pallas_call x1, Pallas kernels: 78 us -> 76.8 us  [body(): pl.pallas_call(kernel, out_shape=jax.ShapeDtypeStruct((TOK // SEQ, SEQ, C...]
where the time goes in v3:
time: 77.9 us; the launch traced here: 77.8 us
  Pallas kernels  76.8 us (99%)
  local copies, waits for them, and re-layouts  0.97 us (1%)
    pallas_call x1, Pallas kernels, body(): pl.pallas_call(kernel, out_shape=jax.ShapeDtypeStruct((TOK // SEQ, SEQ, C...  76.8 us

profile of v3, /device:TPU:1, one launch (start us, length us, event | category | flops | bytes accessed | tf_op | source)
XLA Modules:
  0.0 77.8 jit_solution(14912393869237218265)
XLA Ops:
  0.0 76.8 %shard_map.82 = f32[4,64,1024]{2,1,0:T(8,128)S(1)} custom-call(f32[3,256,1024]{2,1,0:T(8,128)} %streams_hbm.1, f32[3,3,1024]{2,1,0:T(4,128)} %taps_hbm.1, f32[1024]{0:T(1024)} %gain_hbm.1, f32[64,256]{1,0:T(8,128)} %bitcast.1, bf16[128,192]{1,0:T(8,128)(2,1)} %constant.8.clone.head_hbm, bf16[64,384]{1,0:T(8,128)(2,1)} %constant.9.clone.tail_hbm, ...), custom_call_target="tpu_custom_call" | custom-call | tf_op jit(solution)/shard_map/pallas_call | solution.py:537
  76.8 1.0 %copy.10 = f32[4,64,1024]{2,1,0:T(8,128)} copy(f32[4,64,1024]{2,1,0:T(8,128)S(1)} %shard_map.82) | data formatting | bytes 2097152

commit v4 on v3

--- a/solution.py
+++ b/solution.py
@@ -69,7 +69,7 @@
     streams_hbm, taps_hbm, gain_hbm, filter_hbm, head_hbm, tail_hbm, twist_hbm, wide_hbm,
     out_ref,
     stream, taps, gain, filt, head, tail, twist, wide,
-    rim, filt_send, filt_recv, filt_all, response,
+    ends, rim_send, rim, filt_send, filt_recv, filt_all, response,
     gate_send, gate_recv, near_send, near_recv, far_send, far_recv, anti_send, anti_recv,
     own_send, own_recv, conv_send, conv_recv,
     load_sem, rim_sems, filt_sems, ring_sems, gate_out, gate_in, near_sems, far_sems, anti_sems, own_sems,
@@ -109,6 +109,9 @@
     small_loads[0].start()
     for block in range(8):
         query_load(block).start()
+    for block in range(8):
+        last_rows = streams_hbm.at[:, pl.ds(TOK - 8, 8), pl.ds(block * LANES, LANES)]
+        load(last_rows, ends.at[:, block], 23).start()
 
     def greet(step, carry):
         other = lax.rem(me + step, SEQ)
@@ -171,19 +174,16 @@
     for half in range(2):
         filt_send[:, half, :] = filt[:, half * LANES : half * LANES + LANES]
 
+    wait_bytes(ends, load_sem.at[23])
+    rim_send[...] = ends[:, :, 6:8, :]
     pl.semaphore_wait(barrier, SEQ - 1 + GRP - 1)
-
-    def rim_copy(block, other):
-        return pltpu.make_async_remote_copy(
-            src_ref=streams_hbm.at[:, pl.ds(TOK - 8, 8), pl.ds(block * LANES, LANES)],
-            dst_ref=rim.at[:, block], send_sem=rim_sems.at[0], recv_sem=rim_sems.at[1],
-            device_id=(other, group), device_id_type=MESH,
-        )
 
     @pl.when(me < SEQ - 1)
     def _():
-        for block in range(8):
-            rim_copy(block, me + 1).start()
+        pltpu.make_async_remote_copy(
+            src_ref=rim_send, dst_ref=rim, send_sem=rim_sems.at[0], recv_sem=rim_sems.at[1],
+            device_id=(me + 1, group), device_id_type=MESH,
+        ).start()
 
     def near_copy(other):
         return pltpu.make_async_remote_copy(
@@ -238,7 +238,7 @@
     def _():
         wait_bytes(rim, rim_sems.at[1])
         for s in range(3):
-            stream[s, :, pl.ds(6, 2), :] = rim[s, :, pl.ds(6, 2), :]
+            stream[s, :, pl.ds(6, 2), :] = rim[s]
 
     def gate_early(quarter, carry):
         gate(quarter, 0)
@@ -516,7 +516,7 @@
 
     @pl.when(me < SEQ - 1)
     def _():
-        wait_bytes(streams_hbm.at[:, pl.ds(TOK - 8, 8), :], rim_sems.at[0])
+        wait_bytes(rim_send, rim_sems.at[0])
 
     wait_bytes(filt_send.at[pl.ds(0, SEQ - 1)], filt_sems.at[0])
     wait_bytes(filt_all.at[pl.ds(0, GRP - 1)], ring_sems.at[0])
@@ -549,6 +549,8 @@
             pltpu.VMEM(twists.shape, f32),
             pltpu.VMEM(wide.shape, jnp.bfloat16),
             pltpu.VMEM((3, 8, 8, LANES), f32),
+            pltpu.VMEM((3, 8, 2, LANES), f32),
+            pltpu.VMEM((3, 8, 2, LANES), f32),
             pltpu.VMEM((SEQ, 2, LANES), f32),
             pltpu.VMEM((SEQ, 2, LANES), f32),
             pltpu.VMEM((GRP, SEQ, TOK), f32),
@@ -565,7 +567,7 @@
             pltpu.VMEM((SEQ * 16, LANES), f32),
             pltpu.VMEM((QUARTERS, SEQ * 8, LANES), f32),
             pltpu.VMEM((QUARTERS, SEQ * 8, LANES), f32),
-            dma((23,)),
+            dma((24,)),
             dma((2,)),
             dma((2,)),
             dma((2,)),

time: 77.9 us -> 77.1 us (0.990)
  Pallas kernels: 76.8 us -> 76 us
where the time goes in v4:
time: 77.1 us; the launch traced here: 77 us
  Pallas kernels  76 us (99%)
  local copies, waits for them, and re-layouts  0.97 us (1%)
    pallas_call x1, Pallas kernels, body(): pl.pallas_call(kernel, out_shape=jax.ShapeDtypeStruct((TOK // SEQ, SEQ, C...  76 us

profile of v4, /device:TPU:1, one launch (start us, length us, event | category | flops | bytes accessed | tf_op | source)
XLA Modules:
  0.0 77.0 jit_solution(3775745204001355239)
XLA Ops:
  0.0 76.0 %shard_map.82 = f32[4,64,1024]{2,1,0:T(8,128)S(1)} custom-call(f32[3,256,1024]{2,1,0:T(8,128)} %streams_hbm.1, f32[3,3,1024]{2,1,0:T(4,128)} %taps_hbm.1, f32[1024]{0:T(1024)} %gain_hbm.1, f32[64,256]{1,0:T(8,128)} %bitcast.1, bf16[128,192]{1,0:T(8,128)(2,1)} %constant.8.clone.head_hbm, bf16[64,384]{1,0:T(8,128)(2,1)} %constant.9.clone.tail_hbm, ...), custom_call_target="tpu_custom_call" | custom-call | tf_op jit(solution)/shard_map/pallas_call | solution.py:537
  76.1 1.0 %copy.10 = f32[4,64,1024]{2,1,0:T(8,128)} copy(f32[4,64,1024]{2,1,0:T(8,128)S(1)} %shard_map.82) | data formatting | bytes 2097152

commit v5 on v4

--- a/solution.py
+++ b/solution.py
@@ -436,7 +436,7 @@
                 conv_send[quarter, pl.ds(start, 32, 8), :] = flipped[part * 32 : part * 32 + 32]
 
         def send(step, inner):
-            other = lax.rem(me + step, SEQ)
+            other = lax.rem(me + 1 + lax.rem(step + 6, SEQ - 1), SEQ)
             pltpu.make_async_remote_copy(
                 src_ref=conv_send.at[quarter, pl.ds(pl.multiple_of(other * 8, 8), 8)],
                 dst_ref=conv_recv.at[quarter, pl.ds(pl.multiple_of(me * 8, 8), 8)],

time: 77.1 us -> 77 us (level)
  no operation moved by 1% of the time
where the time goes in v5:
time: 77 us; the launch traced here: 76.9 us
  Pallas kernels  75.9 us (99%)
  local copies, waits for them, and re-layouts  0.97 us (1%)
    pallas_call x1, Pallas kernels, body(): pl.pallas_call(kernel, out_shape=jax.ShapeDtypeStruct((TOK // SEQ, SEQ, C...  75.9 us

profile of v5, /device:TPU:1, one launch (start us, length us, event | category | flops | bytes accessed | tf_op | source)
XLA Modules:
  0.0 76.9 jit_solution(13529412889305270958)
XLA Ops:
  0.0 75.9 %shard_map.82 = f32[4,64,1024]{2,1,0:T(8,128)S(1)} custom-call(f32[3,256,1024]{2,1,0:T(8,128)} %streams_hbm.1, f32[3,3,1024]{2,1,0:T(4,128)} %taps_hbm.1, f32[1024]{0:T(1024)} %gain_hbm.1, f32[64,256]{1,0:T(8,128)} %bitcast.1, bf16[128,192]{1,0:T(8,128)(2,1)} %constant.8.clone.head_hbm, bf16[64,384]{1,0:T(8,128)(2,1)} %constant.9.clone.tail_hbm, ...), custom_call_target="tpu_custom_call" | custom-call | tf_op jit(solution)/shard_map/pallas_call | solution.py:537
  75.9 1.0 %copy.10 = f32[4,64,1024]{2,1,0:T(8,128)} copy(f32[4,64,1024]{2,1,0:T(8,128)S(1)} %shard_map.82) | data formatting | bytes 2097152
